TPU v7x, 32 devices: a whole 2x2x4 slice. The times are simulated.
32 devices in a mesh: grp: 2 (over y), lib: 4 (over x, core), ptl: 4 (over z).
Axes of the slice: x: 2, y: 2, z: 4, core: 2. Of those that a mesh axis runs over, the one named last changes fastest.
Arguments:
- particles: bfloat16 [1536, 9984], P(('grp', 'lib', 'ptl')), parts along dimension 0
- shifts: int32 [1536], P(('grp', 'lib', 'ptl')), parts along dimension 0, may hold values from 0 to 8
- references: bfloat16 [1024, 9984], P(('grp', 'lib')), parts along dimension 0
- inv_noise: float32 [9984], P('grp'), parts along dimension 0, may hold values from 0.015024038 to 0.060096152
- proj_class: int32 [512], P('lib'), may hold values from 0 to 15
Outputs:
- log_evidence: float32 [1536], P(('grp', 'lib', 'ptl')), parts along dimension 0
- class_posterior: float32 [1536, 16], P(('grp', 'lib', 'ptl')), parts along dimension 0
- weighted_sums: float32 [1024, 9984], P(('grp', 'lib'), 'ptl'), parts along dimension 0
- weight_totals: float32 [1024], P(('grp', 'lib', 'ptl')), parts along dimension 0
There are 2 independent parts, one for each index of `grp`. A program takes and returns all parts, laid end to end along the dimension named above; an argument that names none is the same for every part. Nothing has to cross between parts.
All inputs are finite; a program needn't handle non-finite values.
Results may differ from a plain program's by a relative error of at most 0.0085.
Values may be sent and summed in bfloat16 or wider, within the bound.
A program may use at most 64 MiB of HBM per device.

v0:
```python
import math

import jax
import jax.numpy as jnp
from jax import lax
from jax.sharding import PartitionSpec as P

CLASSES = 16


def shift_images(images, shift_ids):
    half_width = images.shape[1] // 2
    freq_index = jnp.arange(half_width, dtype=jnp.int32)
    freq_x = (freq_index % 64).astype(jnp.float32)
    freq_y = (freq_index // 64).astype(jnp.float32)
    step_x = (shift_ids % 3 - 1).astype(jnp.float32)
    step_y = (shift_ids // 3 - 1).astype(jnp.float32)
    angle = (step_x[:, None] * freq_x[None, :] + step_y[:, None] * freq_y[None, :]) * (
        2.0 * math.pi / 128.0
    )
    cosine = jnp.cos(angle)
    sine = jnp.sin(angle)
    real_part = images[:, :half_width].astype(jnp.float32)
    imag_part = images[:, half_width:].astype(jnp.float32)
    return jnp.concatenate(
        [real_part * cosine + imag_part * sine, imag_part * cosine - real_part * sine], axis=1
    ).astype(jnp.bfloat16)


def prepare_refs(references, inv_noise):
    doubled = jnp.concatenate([inv_noise, inv_noise])
    widened = references.astype(jnp.float32)
    weighted = (widened * doubled[None, :]).astype(jnp.bfloat16)
    half_norm = 0.5 * jnp.sum(widened * widened * doubled[None, :], axis=1)
    return (weighted, half_norm)


def score_rows(rows, weighted, half_norm):
    return (
        lax.dot_general(
            rows, weighted, (((1,), (1,)), ((), ())), preferred_element_type=jnp.float32
        )
        - half_norm[None, :]
    )


def weigh_rows(post_weights, rows):
    return lax.dot_general(
        post_weights, rows, (((0,), (0,)), ((), ())), preferred_element_type=jnp.float32
    )


def on_device(particles, shifts, references, inv_noise, proj_class):
    shifted = shift_images(particles, shifts)
    weighted, half_norm = prepare_refs(references, inv_noise)
    onehot = (proj_class[:, None] == jnp.arange(CLASSES, dtype=jnp.int32)[None, :]).astype(
        jnp.bfloat16
    )
    gathered = lax.all_gather(shifted, "lib", axis=0, tiled=True)
    scores = score_rows(gathered, weighted, half_norm)
    peak = lax.pmax(jnp.max(scores, axis=1), "lib")
    total = lax.psum(jnp.sum(jnp.exp(scores - peak[:, None]), axis=1), "lib")
    evidence = peak + jnp.log(total)
    post_weights = jnp.exp(scores - evidence[:, None]).astype(jnp.bfloat16)
    shares = lax.psum_scatter(
        jnp.dot(post_weights, onehot, preferred_element_type=jnp.float32).astype(jnp.bfloat16),
        "lib",
        scatter_dimension=0,
        tiled=True,
    ).astype(jnp.float32)
    own_rows = particles.shape[0]
    own_evidence = lax.dynamic_slice_in_dim(evidence, lax.axis_index("lib") * own_rows, own_rows, 0)
    sums = weigh_rows(post_weights, gathered)
    totals = jnp.sum(post_weights.astype(jnp.float32), axis=0)
    out_sums, out_totals = (
        lax.psum_scatter(sums.astype(jnp.bfloat16), "ptl", scatter_dimension=1, tiled=True).astype(
            jnp.float32
        ),
        lax.psum_scatter(
            totals.astype(jnp.bfloat16), "ptl", scatter_dimension=0, tiled=True
        ).astype(jnp.float32),
    )
    return (own_evidence, shares, out_sums, out_totals)


def solution(mesh):
    in_specs = (
        P(("grp", "lib", "ptl"), None),
        P(("grp", "lib", "ptl")),
        P(("grp", "lib"), None),
        P("grp"),
        P("lib"),
    )
    out_specs = (
        P(("grp", "lib", "ptl")),
        P(("grp", "lib", "ptl"), None),
        P(("grp", "lib"), "ptl"),
        P(("grp", "lib", "ptl")),
    )
    return jax.shard_map(
        on_device, mesh=mesh, in_specs=in_specs, out_specs=out_specs, check_vma=False
    )
```

profile of v0, /device:TPU:0, one launch (start us, length us, event | category | flops | bytes accessed | tf_op | source)
XLA Modules:
  0.0 149.5 jit_solution(9254654302861352949)
XLA Ops:
  7.2 0.0 copy-start.1
  7.2 0.0 copy-start
  7.2 0.0 all-gather.2.cloned.1.call-start
  7.2 0.8 fusion.24
  8.1 5.7 %fusion.10 = (bf16[48,4992]{1,0:T(8,128)(2,1)S(1)}, bf16[48,4992]{1,0:T(8,128)(2,1)S(1)}) fusion(f32[4992]{0:T(1024)S(1)} %get-tuple-element.13, f32[48]{0:T(128)S(1)} %get-tuple-element.9, f32[4992]{0:T(1024)S(1)} %get-tuple-element.12, f32[48]{0:T(128)S(1)} %get-tuple-element.8, bf16[48,9984]{1,0:T(8,128)(2,1)} %param.5), kind=kLoop, calls=%fused_computation.15 | loop fusion | flops 3354624 | bytes 1957248 | tf_op jit(solution)/shard_map/convert.1
  13.8 1.0 pad_maximum_fusion
  14.8 0.0 all-gather.2.cloned.1.call-update
  14.8 0.0 reduce-scatter.7.cloned.1.call-start
  14.8 0.0 copy-done.1
  14.9 0.0 copy-done
  14.9 0.8 fusion.2
  15.6 0.0 copy-start.2
  15.6 34.4 %all-gather.2.cloned.1.call-done = bf16[192,9984]{1,0:T(8,128)(2,1)} async-done(((bf16[48,9984]{1,0:T(8,128)(2,1)}), bf16[192,9984]{1,0:T(8,128)(2,1)}) %all-gather.2.cloned.1.call-update) | async-done | bytes 3833872 | tf_op jit(solution)/shard_map/all_gather | solution.py:59
  50.1 3.3 %fusion.26 = (f32[192]{0:T(256)S(1)}, f32[192,128]{1,0:T(8,128)S(1)}) fusion(f32[128]{0:T(128)S(1)} %broadcast_multiply_fusion, bf16[192,9984]{1,0:T(8,128)(2,1)} %all-gather.2.cloned.1.call-done, bf16[128,9984]{1,0:T(8,128)(2,1)S(1)} %copy-done, f32[9984]{0:T(1024)S(1)} %pad_maximum_fusion.1), kind=kOutput, calls=%fused_computation.48 | convolution fusion | flops 494616384 | bytes 6529280 | tf_op jit(solution)/shard_map/dot_general | solution.py:40
  53.4 5.9 %pmax.7 = f32[192]{0:T(256)S(1)} all-reduce(f32[192]{0:T(256)S(1)} %get-tuple-element.10), channel_id=1, replica_groups=mesh['grp'=2,'lib'=4,'ptl'=4] {'lib'}, use_global_device_ids=true, to_apply=%region_2.3 | all-reduce | flops 192 | bytes 1536 | tf_op jit(solution)/shard_map/pmax | solution.py:61
  59.3 0.2 exponential_reduce_fusion
  59.5 5.7 %psum.7 = f32[192]{0:T(256)S(1)} all-reduce(f32[192]{0:T(256)S(1)} %exponential_reduce_fusion), channel_id=1, replica_groups=mesh['grp'=2,'lib'=4,'ptl'=4] {'lib'}, use_global_device_ids=true, to_apply=%region_4.5 | all-reduce | flops 192 | bytes 1536 | tf_op jit(solution)/shard_map/psum | solution.py:62
  65.2 0.1 fusion.25
  65.3 0.0 copy-done.2
  65.3 0.2 convolution_convert_fusion.1
  65.6 0.7 copy.9
  66.3 0.0 reduce-scatter.7.cloned.1.call-update
  66.3 0.0 copy-start.3
  66.3 0.0 reduce-scatter.5.cloned.1.call-start
  66.4 5.7 %convolution_convert_fusion = bf16[128,9984]{0,1:T(8,128)(2,1)} fusion(bf16[192,128]{1,0:T(8,128)(2,1)S(1)} %get-tuple-element.5, bf16[192,9984]{1,0:T(8,128)(2,1)} %all-gather.2.cloned.1.call-done), kind=kOutput, calls=%fused_computation | convolution fusion | flops 492011520 | bytes 6438912 | tf_op jit(solution)/shard_map/dot_general | solution.py:48
  72.0 0.0 reduce-scatter.5.cloned.1.call-update
  72.1 0.0 copy-done.3
  72.1 0.6 dynamic-slice
  73.3 0.6 dynamic_slice.3
  73.9 11.8 %all-reduce = bf16[128]{0:T(256)(128)(2,1)S(1)} all-reduce(bf16[128]{0:T(256)(128)(2,1)S(1)} %get-tuple-element.4), channel_id=4, replica_groups=mesh['grp'=2,'lib'=4,'ptl'=4] {'ptl'}, use_global_device_ids=true, to_apply=%region_8.9.clone | all-reduce | flops 128 | bytes 512
  85.7 0.6 dynamic-slice_convert_fusion
  86.3 0.9 reduce-scatter.7.cloned.1.call-done
  87.2 0.8 copy.10
  88.0 0.6 convert_element_type.64
  88.6 52.2 %reduce-scatter.5.cloned.1.call-done = bf16[128,2496]{0,1:T(8,128)(2,1)} async-done(((bf16[128,9984]{0,1:T(8,128)(2,1)}), bf16[128,2496]{0,1:T(8,128)(2,1)}) %reduce-scatter.5.cloned.1.call-update) | async-done | bytes 638992 | tf_op jit(solution)/shard_map/reduce_scatter | solution.py:76
  140.8 2.2 %convert_element_type.66 = f32[128,2496]{0,1:T(8,128)} convert(bf16[128,2496]{0,1:T(8,128)(2,1)} %reduce-scatter.5.cloned.1.call-done) | non-fusion elementwise | flops 319488 | bytes 1916928 | tf_op jit(solution)/shard_map/convert_element_type | solution.py:76
  (4 shorter events, 0.0 us)
Async XLA Ops:
  7.2 7.7 %copy-start.1 = (f32[4992]{0:T(1024)S(1)}, f32[4992]{0:T(1024)}, u32[]{:S(2)}) copy-start(f32[4992]{0:T(1024)} %param.8) | copy-start | bytes 59908
  7.2 7.7 %copy-start = (bf16[128,9984]{1,0:T(8,128)(2,1)S(1)}, bf16[128,9984]{1,0:T(8,128)(2,1)}, u32[]{:S(2)}) copy-start(bf16[128,9984]{1,0:T(8,128)(2,1)} %param.7) | copy-start | bytes 7667716
  7.2 42.9 %all-gather.2.cloned.1.call-start = ((), (), s32[]{:S(2)}) async-start(), calls=%async_computation.2 | async-start | bytes 4792320 | tf_op jit(solution)/shard_map/all_gather | solution.py:59
  14.8 72.4 %reduce-scatter.7.cloned.1.call-start = ((), (), s32[]{:S(2)}) async-start(), calls=%async_computation.4 | async-start | bytes 61440
  15.6 49.7 %copy-start.2 = (s32[128]{0:T(128)S(1)}, s32[128]{0:T(128)}, u32[]{:S(2)}) copy-start(s32[128]{0:T(128)} %param.9) | copy-start | bytes 1540
  66.3 5.8 %copy-start.3 = (u32[32]{0:T(128)S(1)}, u32[32]{0:T(128)}, u32[]{:S(2)}) copy-start(u32[32]{0:T(128)} %constant.75) | copy-start | bytes 388
  66.3 74.4 %reduce-scatter.5.cloned.1.call-start = ((), (), s32[]{:S(2)}) async-start(), calls=%async_computation.3 | async-start | bytes 3194880 | tf_op jit(solution)/shard_map/reduce_scatter | solution.py:76
Sparse Core Ops, SparseCore 0:
  14.9 35.1 all-gather.1
  66.4 20.7 reduce-scatter.6
  89.6 51.0 reduce-scatter.4
where the time goes:
time: 150 us
  waiting for transfers between devices  87.5 us (58%)
  blocking collectives  23.4 us (16%)
  between operations  14.5 us (10%)
  other arithmetic  12 us (8%)
  matrix products  9.23 us (6%)
  local copies, waits for them, and re-layouts  2.71 us (2%)
    reduce_scatter x1, waiting for transfers between devices, on_device(): lax.psum_scatter(sums.astype(jnp.bfloat16), 'ptl', scatter_dimension=1, t...  52.2 us
    all_gather x1, waiting for transfers between devices, on_device(): gathered = lax.all_gather(shifted, 'lib', axis=0, tiled=True)  34.4 us
    unnamed x1, blocking collectives  11.8 us
    pmax x1, blocking collectives, on_device(): peak = lax.pmax(jnp.max(scores, axis=1), 'lib')  5.91 us
    another operation x1, other arithmetic  5.68 us
    psum x1, blocking collectives, on_device(): total = lax.psum(jnp.sum(jnp.exp(scores - peak[:, None]), axis=1), 'lib')  5.67 us
    dot_general x1, matrix products, weigh_rows(): lax.dot_general(post_weights, rows, (((0,), (0,)), ((), ())), preferred_e...  5.66 us
    dot_general x1, matrix products, score_rows(): lax.dot_general(rows, weighted, (((1,), (1,)), ((), ())), preferred_eleme...  3.33 us
  transfers between devices with their start and end apart: 3, of which 3 were waited for; matrix products, arithmetic and copies ran while one was open for 6% of the time, Pallas kernels for 0%

commit v1 on v0

v1 whole, which is shorter than its diff:
```python
import functools
import math

import jax
import jax.numpy as jnp
import numpy as np
from jax import lax
from jax.experimental import pallas as pl
from jax.experimental.pallas import tpu as pltpu
from jax.sharding import PartitionSpec as P

CLASSES = 16
LANES = 128


def run_loop(low, high, body):
    if high - low <= 4:
        for index in range(low, high):
            body(index)
    else:

        def step(index, carry):
            body(index)
            return carry

        lax.fori_loop(low, high, step, 0)


def hop(index, count):
    odd = index % 2
    return odd * ((index + 1) // 2) + (1 - odd) * (count - index // 2)


def kernel(
    n_lib,
    n_ptl,
    span,
    part_ref,
    shift_ref,
    table_ref,
    refs_hbm,
    noise_ref,
    class_ref,
    sums_ref,
    evid_ref,
    share_ref,
    total_ref,
    shifted,
    gath,
    refbuf,
    weighted,
    spart,
    srecv,
    post,
    stat,
    stat_in,
    share_out,
    share_in,
    totbuf,
    ref_sem,
    own_sem,
    z_send,
    z_recv,
    x_send,
    x_recv,
    c_send,
    c_recv,
    s_send,
    s_recv,
    t_send,
    t_recv,
    p_send,
    p_recv,
    h_send,
    h_recv,
):
    lib = lax.axis_index("lib")
    ptl = lax.axis_index("ptl")
    n_x = n_lib // 2
    x, core = lib // 2, lib % 2
    mate = 2 * x + 1 - core
    rows, width = part_ref.shape
    half = width // 2
    part_cols = width // n_ptl
    tiles = width // LANES

    def first_tile(z):
        return jnp.minimum((z * part_cols) // LANES, tiles - span // LANES)

    def chunk(z):
        return pl.ds(pl.multiple_of(first_tile(z) * LANES, LANES), span)

    barrier = pltpu.get_barrier_semaphore()

    def greet_ptl(step):
        pl.semaphore_signal(barrier, inc=1, device_id={"ptl": lax.rem(ptl + step, n_ptl)})

    def greet_lib(step):
        pl.semaphore_signal(barrier, inc=1, device_id={"lib": lax.rem(lib + step, n_lib)})

    run_loop(1, n_ptl, greet_ptl)
    run_loop(1, n_lib, greet_lib)

    ref_copy = pltpu.make_async_copy(refs_hbm.at[:, chunk(ptl)], refbuf, ref_sem)
    ref_copy.start()

    ids = shift_ref[...]
    step_y = (ids >= 3).astype(jnp.int32) + (ids >= 6).astype(jnp.int32)
    step_x = (ids - 3 * step_y - 1).astype(jnp.float32)
    step_y = (step_y - 1).astype(jnp.float32)
    cos_x = jnp.where(step_x == 0.0, 1.0, table_ref[0:1, 0:LANES])
    sin_x = step_x * table_ref[1:2, 0:LANES]
    for tile in range(half // LANES):
        lo = slice(tile * LANES, (tile + 1) * LANES)
        hi = slice(half + tile * LANES, half + (tile + 1) * LANES)
        cos_y = jnp.where(step_y == 0.0, 1.0, table_ref[2:3, lo])
        sin_y = step_y * table_ref[3:4, lo]
        cosine = cos_x * cos_y - sin_x * sin_y
        sine = sin_x * cos_y + cos_x * sin_y
        real = part_ref[:, lo].astype(jnp.float32)
        imag = part_ref[:, hi].astype(jnp.float32)
        shifted[:, lo] = (real * cosine + imag * sine).astype(jnp.bfloat16)
        shifted[:, hi] = (imag * cosine - real * sine).astype(jnp.bfloat16)

    pl.semaphore_wait(barrier, n_ptl - 1 + n_lib - 1)

    def z_copy(i):
        to = lax.rem(ptl + hop(i, n_ptl), n_ptl)
        return pltpu.make_async_remote_copy(
            src_ref=shifted.at[:, chunk(to)],
            dst_ref=gath.at[i, lib],
            send_sem=z_send.at[i - 1],
            recv_sem=z_recv.at[i - 1],
            device_id={"ptl": to},
        )

    run_loop(1, n_ptl, lambda i: z_copy(i).start())
    own_copy = pltpu.make_async_copy(shifted.at[:, chunk(ptl)], gath.at[0, lib], own_sem)
    own_copy.start()

    def x_copy(i, d):
        return pltpu.make_async_remote_copy(
            src_ref=gath.at[i, lib],
            dst_ref=gath.at[i, lib],
            send_sem=x_send.at[i, d - 1],
            recv_sem=x_recv.at[i, d - 1],
            device_id={"lib": lax.rem(x + d, n_x) * 2 + core},
        )

    def x_arrival(i, d):
        source = lax.rem(x - d + n_x, n_x) * 2 + core
        return pltpu.make_async_remote_copy(
            src_ref=gath.at[i, source],
            dst_ref=gath.at[i, source],
            send_sem=x_send.at[i, d - 1],
            recv_sem=x_recv.at[i, d - 1],
            device_id={"lib": source},
        )

    def core_copy(i, d):
        source = lax.rem(x - d + n_x, n_x) * 2 + core
        return pltpu.make_async_remote_copy(
            src_ref=gath.at[i, source],
            dst_ref=gath.at[i, source],
            send_sem=c_send.at[i, d],
            recv_sem=c_recv.at[i, d],
            device_id={"lib": mate},
        )

    def core_arrival(i, d):
        source = lax.rem(x - d + n_x, n_x) * 2 + 1 - core
        return pltpu.make_async_remote_copy(
            src_ref=gath.at[i, source],
            dst_ref=gath.at[i, source],
            send_sem=c_send.at[i, d],
            recv_sem=c_recv.at[i, d],
            device_id={"lib": mate},
        )

    def z_arrival(i):
        source = lax.rem(ptl - hop(i, n_ptl) + n_ptl, n_ptl)
        return pltpu.make_async_remote_copy(
            src_ref=shifted.at[:, chunk(ptl)],
            dst_ref=gath.at[i, lib],
            send_sem=z_send.at[i - 1],
            recv_sem=z_recv.at[i - 1],
            device_id={"ptl": source},
        )

    def spread(i):
        run_loop(1, n_x, lambda d: x_copy(i, d).start())
        core_copy(i, 0).start()

    def score_copy(i):
        return pltpu.make_async_remote_copy(
            src_ref=spart.at[i],
            dst_ref=srecv.at[i - 1],
            send_sem=s_send.at[i - 1],
            recv_sem=s_recv.at[i - 1],
            device_id={"ptl": lax.rem(ptl - hop(i, n_ptl) + n_ptl, n_ptl)},
        )

    def relay(i):
        def forward(d):
            x_arrival(i, d).wait_recv()
            core_copy(i, d).start()

        run_loop(1, n_x, forward)
        run_loop(0, n_x, lambda d: core_arrival(i, d).wait_recv())

    def score(i):
        block = gath[i].reshape(n_lib * rows, span)
        spart[i] = (
            lax.dot_general(
                weighted[...], block, (((1,), (1,)), ((), ())), preferred_element_type=jnp.float32
            )
            - half_norm
        )

    own_copy.wait()
    spread(0)

    ref_copy.wait()
    offset = ptl * part_cols - first_tile(ptl) * LANES
    place = lax.broadcasted_iota(jnp.int32, (1, span), 1)
    inside = (place >= offset) & (place < offset + part_cols)
    noise = jnp.where(inside, noise_ref[:, chunk(ptl)], 0.0)
    widened = refbuf[...].astype(jnp.float32)
    scaled = widened * noise
    weighted[...] = scaled.astype(jnp.bfloat16)
    half_norm = 0.5 * jnp.sum(widened * scaled, axis=1, keepdims=True)

    def advance(i):
        z_arrival(i).wait_recv()
        spread(i)
        relay(i - 1)
        score(i - 1)

    z_arrival(1).wait_recv()
    spread(1)
    relay(0)
    score(0)

    def middle(i):
        advance(i)
        score_copy(i - 1).start()

    run_loop(2, n_ptl, middle)
    relay(n_ptl - 1)
    score(n_ptl - 1)
    score_copy(n_ptl - 1).start()

    def add_scores(i):
        score_copy(i).wait_recv()
        spart[0] = spart[0] + srecv[i - 1]

    run_loop(1, n_ptl, add_scores)
    scores = spart[0]

    peak = jnp.max(scores, axis=0, keepdims=True)
    stat[0:1] = peak
    stat[1:2] = jnp.sum(jnp.exp(scores - peak), axis=0, keepdims=True)

    def stat_copy(d):
        return pltpu.make_async_remote_copy(
            src_ref=stat,
            dst_ref=stat_in.at[d],
            send_sem=t_send.at[d - 1],
            recv_sem=t_recv.at[d - 1],
            device_id={"lib": lax.rem(lib + d, n_lib)},
        )

    run_loop(1, n_lib, lambda d: stat_copy(d).start())
    stat_in[0, 0:2] = stat[0:2]
    run_loop(1, n_lib, lambda d: stat_copy(d).wait_recv())
    top = peak
    for d in range(1, n_lib):
        top = jnp.maximum(top, stat_in[d, 0:1])
    total = jnp.zeros_like(top)
    for d in range(n_lib):
        total = total + stat_in[d, 1:2] * jnp.exp(stat_in[d, 0:1] - top)
    evidence = top + jnp.log(total)
    evid_ref[...] = evidence
    own_post = jnp.exp(scores - evidence).astype(jnp.bfloat16)
    post[0] = own_post

    def post_copy(i):
        return pltpu.make_async_remote_copy(
            src_ref=post.at[0],
            dst_ref=post.at[i],
            send_sem=p_send.at[i - 1],
            recv_sem=p_recv.at[i - 1],
            device_id={"ptl": lax.rem(ptl + hop(i, n_ptl), n_ptl)},
        )

    run_loop(1, n_ptl, lambda i: post_copy(i).start())

    onehot = (
        class_ref[...] == lax.broadcasted_iota(jnp.int32, (class_ref.shape[0], CLASSES), 1)
    ).astype(jnp.bfloat16)
    share_out[...] = lax.dot_general(
        own_post, onehot, (((0,), (0,)), ((), ())), preferred_element_type=jnp.float32
    ).reshape(n_lib, rows, CLASSES)

    def share_copy(d):
        to = lax.rem(lib + d, n_lib)
        return pltpu.make_async_remote_copy(
            src_ref=share_out.at[to],
            dst_ref=share_in.at[d - 1],
            send_sem=h_send.at[d - 1],
            recv_sem=h_recv.at[d - 1],
            device_id={"lib": to},
        )

    run_loop(1, n_lib, lambda d: share_copy(d).start())

    block = 512 if span % 512 == 0 else LANES

    def own_sums(b):
        cols = pl.ds(pl.multiple_of(b * block, block), block)
        images = gath[0, :, :, cols].reshape(n_lib * rows, block)
        sums_ref[:, cols] = jnp.dot(own_post, images, preferred_element_type=jnp.float32)

    lax.fori_loop(0, span // block, lambda b, c: (own_sums(b), c)[1], 0)

    totbuf[...] = jnp.sum(own_post.astype(jnp.float32), axis=1, keepdims=True)
    run_loop(1, n_ptl, lambda i: post_copy(i).wait_recv())

    def add_total(i):
        totbuf[...] += jnp.sum(post[i].astype(jnp.float32), axis=1, keepdims=True)

    run_loop(1, n_ptl, add_total)

    def other_sums(b):
        cols = pl.ds(pl.multiple_of(b * block, block), block)
        sums = sums_ref[:, cols]
        for i in range(1, n_ptl):
            images = gath[i, :, :, cols].reshape(n_lib * rows, block)
            sums = sums + jnp.dot(post[i], images, preferred_element_type=jnp.float32)
        sums_ref[:, cols] = sums

    lax.fori_loop(0, span // block, lambda b, c: (other_sums(b), c)[1], 0)

    own_total = total_ref.shape[0]
    total_ref[...] = totbuf[pl.ds(pl.multiple_of(ptl * own_total, 8), own_total), :]

    share = share_out[lib]
    for d in range(1, n_lib):
        share_copy(d).wait_recv()
        share = share + share_in[d - 1]
    share_ref[...] = share

    def ptl_sent(i):
        z_copy(i).wait_send()
        score_copy(i).wait_send()
        post_copy(i).wait_send()

    def lib_sent(d):
        stat_copy(d).wait_send()
        share_copy(d).wait_send()

    def spread_sent(i):
        run_loop(1, n_x, lambda d: x_copy(i, d).wait_send())
        run_loop(0, n_x, lambda d: core_copy(i, d).wait_send())

    run_loop(1, n_ptl, ptl_sent)
    run_loop(1, n_lib, lib_sent)
    run_loop(0, n_ptl, spread_sent)


def trig_table(half):
    index = np.arange(half)
    angle_x = (index % 64) * (2.0 * math.pi / 128.0)
    angle_y = (index // 64) * (2.0 * math.pi / 128.0)
    table = np.zeros((8, half), np.float32)
    table[0], table[1] = np.cos(angle_x), np.sin(angle_x)
    table[2], table[3] = np.cos(angle_y), np.sin(angle_y)
    return table


def on_device(n_lib, n_ptl, particles, shifts, references, inv_noise, proj_class):
    rows, width = particles.shape
    projections = references.shape[0]
    part_cols = width // n_ptl
    tiles = width // LANES
    cover = max(-(-(z * part_cols % LANES + part_cols) // LANES) for z in range(n_ptl))
    span = min(cover, tiles) * LANES
    n_x = n_lib // 2
    group = n_lib * rows
    own_total = projections // n_ptl
    vmem = pl.BlockSpec(memory_space=pltpu.VMEM)
    dma = pltpu.SemaphoreType.DMA
    sums, evidence, share, total = pl.pallas_call(
        functools.partial(kernel, n_lib, n_ptl, span),
        out_shape=(
            jax.ShapeDtypeStruct((projections, span), jnp.float32),
            jax.ShapeDtypeStruct((1, group), jnp.float32),
            jax.ShapeDtypeStruct((rows, CLASSES), jnp.float32),
            jax.ShapeDtypeStruct((own_total, 1), jnp.float32),
        ),
        in_specs=[vmem, vmem, vmem, pl.BlockSpec(memory_space=pl.ANY), vmem, vmem],
        out_specs=(vmem, vmem, vmem, vmem),
        scratch_shapes=[
            pltpu.VMEM((rows, width), jnp.bfloat16),
            pltpu.VMEM((n_ptl, n_lib, rows, span), jnp.bfloat16),
            pltpu.VMEM((projections, span), jnp.bfloat16),
            pltpu.VMEM((projections, span), jnp.bfloat16),
            pltpu.VMEM((n_ptl, projections, group), jnp.float32),
            pltpu.VMEM((n_ptl - 1, projections, group), jnp.float32),
            pltpu.VMEM((n_ptl, projections, group), jnp.bfloat16),
            pltpu.VMEM((8, group), jnp.float32),
            pltpu.VMEM((n_lib, 8, group), jnp.float32),
            pltpu.VMEM((n_lib, rows, CLASSES), jnp.float32),
            pltpu.VMEM((n_lib - 1, rows, CLASSES), jnp.float32),
            pltpu.VMEM((projections, 1), jnp.float32),
            dma,
            dma,
            dma((n_ptl - 1,)),
            dma((n_ptl - 1,)),
            dma((n_ptl, n_x - 1)),
            dma((n_ptl, n_x - 1)),
            dma((n_ptl, n_x)),
            dma((n_ptl, n_x)),
            dma((n_ptl - 1,)),
            dma((n_ptl - 1,)),
            dma((n_lib - 1,)),
            dma((n_lib - 1,)),
            dma((n_ptl - 1,)),
            dma((n_ptl - 1,)),
            dma((n_lib - 1,)),
            dma((n_lib - 1,)),
        ],
        compiler_params=pltpu.CompilerParams(
            collective_id=0, has_side_effects=True, vmem_limit_bytes=56 * 1024 * 1024
        ),
    )(
        particles,
        shifts[:, None],
        trig_table(width // 2),
        references,
        jnp.concatenate([inv_noise, inv_noise])[None, :],
        proj_class[:, None],
    )
    ptl, lib = lax.axis_index("ptl"), lax.axis_index("lib")
    first = jnp.minimum((ptl * part_cols) // LANES, tiles - span // LANES) * LANES
    out_sums = lax.dynamic_slice_in_dim(sums, ptl * part_cols - first, part_cols, 1)
    own_evidence = lax.dynamic_slice_in_dim(evidence[0], lib * rows, rows, 0)
    return own_evidence, share, out_sums, total[:, 0]


def solution(mesh):
    in_specs = (
        P(("grp", "lib", "ptl"), None),
        P(("grp", "lib", "ptl")),
        P(("grp", "lib"), None),
        P("grp"),
        P("lib"),
    )
    out_specs = (
        P(("grp", "lib", "ptl")),
        P(("grp", "lib", "ptl"), None),
        P(("grp", "lib"), "ptl"),
        P(("grp", "lib", "ptl")),
    )
    return jax.shard_map(
        functools.partial(on_device, mesh.shape["lib"], mesh.shape["ptl"]),
        mesh=mesh,
        in_specs=in_specs,
        out_specs=out_specs,
        check_vma=False,
    )
```

time: 150 us -> 72.7 us (0.48)
  the two profiles are of different devices: /device:TPU:0 before, /device:TPU:18 now
where the time goes in v1:
time: 72.7 us; the launch traced here: 72.4 us
  Pallas kernels  60.3 us (83%)
  local copies, waits for them, and re-layouts  9.19 us (13%)
  other arithmetic  2.15 us (3%)
    pallas_call x1, Pallas kernels, on_device(): pl.pallas_call(functools.partial(kernel, n_lib, n_ptl, span), out_shape=(...  60.3 us
    unnamed x2, local copies, waits for them, and re-layouts  2.86 us
    dynamic_slice x1, local copies, waits for them, and re-layouts, on_device(): lax.dynamic_slice_in_dim(sums, ptl * part_cols - first, part_cols, 1)  1.71 us

profile of v1, /device:TPU:18, one launch (start us, length us, event | category | flops | bytes accessed | tf_op | source)
XLA Modules:
  0.0 72.4 jit_solution(6544509089017473325)
XLA Ops:
  0.7 1.3 %copy.14.shift_ref = s32[48,1]{1,0:T(8,128)} copy(s32[48,1]{0,1:T(1,128)} %bitcast.5) | data formatting | bytes 384 | tf_op jit(solution)/shard_map/broadcast_in_dim | solution.py:438
  2.0 0.8 %pad_maximum_fusion = f32[9984]{0:T(1024)S(1)} fusion(f32[4992]{0:T(1024)} %param.9), kind=kLoop, calls=%fused_computation | loop fusion | flops 9984 | bytes 59904 | tf_op jit(solution)/shard_map/concatenate | solution.py:441
  2.8 0.6 broadcast_in_dim.10.noise_ref
  3.4 1.4 %copy.15.class_ref = s32[128,1]{1,0:T(8,128)} copy(s32[128,1]{0,1:T(1,128)} %bitcast.4) | data formatting | bytes 1024 | tf_op jit(solution)/shard_map/broadcast_in_dim | solution.py:442
  4.8 60.3 %shard_map.93 = (f32[128,2560]{1,0:T(8,128)}, f32[1,192]{1,0:T(1,128)}, f32[48,16]{1,0:T(8,128)}, f32[32,1]{1,0:T(8,128)}) custom-call(bf16[48,9984]{1,0:T(8,128)(2,1)} %part_ref.1, s32[48,1]{1,0:T(8,128)} %copy.14.shift_ref, f32[8,4992]{1,0:T(8,128)} %constant.38.clone.table_ref, bf16[128,9984]{1,0:T(8,128)(2,1)} %refs_hbm.1, ...), custom_call_target="tpu_custom_call" | custom-call | tf_op jit(solution)/shard_map/pallas_call | solution.py:393
  65.2 1.3 %dynamic-slice_bitcast_fusion = f32[48]{0:T(128)} fusion(f32[1,192]{1,0:T(1,128)} %get-tuple-element.8, s32[]{:T(128)S(6)} %select_n.11), kind=kLoop, calls=%fused_computation.1 | loop fusion | bytes 388 | tf_op jit(solution)/shard_map/dynamic_slice | solution.py:447
  66.4 1.3 %reduce = f32[32]{0:T(128)} reduce(f32[32,1]{1,0:T(8,128)} %get-tuple-element.11, f32[]{:T(128)} %constant.41), dimensions={1}, to_apply=%get-tuple-element.11.reduce_sub_computation | reduce | bytes 260 | tf_op jit(solution)/shard_map/pallas_call | solution.py:393
  67.8 1.4 %copy.16 = f32[48,16]{0,1:T(8,128)} copy(f32[48,16]{1,0:T(8,128)} %get-tuple-element.17) | data formatting | bytes 6144
  69.2 1.7 %constant_dynamic-slice_fusion = f32[128,2496]{1,0:T(8,128)S(1)} fusion(f32[128,2560]{1,0:T(8,128)} %get-tuple-element.10, s32[]{:T(128)S(6)} %select_n.13), kind=kLoop, calls=%fused_computation.2 | loop fusion | bytes 2555908 | tf_op jit(solution)/shard_map/dynamic_slice | solution.py:446
  70.9 1.5 %copy.17 = f32[128,2496]{0,1:T(8,128)} copy(f32[128,2496]{1,0:T(8,128)S(1)} %constant_dynamic-slice_fusion) | data formatting | bytes 2555904

commit v2 on v1

--- a/solution.py
+++ b/solution.py
@@ -10,6 +10,7 @@
 from jax.sharding import PartitionSpec as P
 
 CLASSES = 16
+WINDOW = 3
 LANES = 128
 
 
@@ -26,15 +27,12 @@
         lax.fori_loop(low, high, step, 0)
 
 
-def hop(index, count):
-    odd = index % 2
-    return odd * ((index + 1) // 2) + (1 - odd) * (count - index // 2)
-
-
 def kernel(
     n_lib,
     n_ptl,
     span,
+    pieces,
+    window,
     part_ref,
     shift_ref,
     table_ref,
@@ -45,6 +43,7 @@
     evid_ref,
     share_ref,
     total_ref,
+    noise2,
     shifted,
     gath,
     refbuf,
@@ -83,6 +82,8 @@
     half = width // 2
     part_cols = width // n_ptl
     tiles = width // LANES
+    piece_rows = rows // pieces
+    n_pieces = n_ptl * pieces
 
     def first_tile(z):
         return jnp.minimum((z * part_cols) // LANES, tiles - span // LANES)
@@ -104,7 +105,12 @@
     ref_copy = pltpu.make_async_copy(refs_hbm.at[:, chunk(ptl)], refbuf, ref_sem)
     ref_copy.start()
 
-    ids = shift_ref[...]
+    same = lax.broadcasted_iota(jnp.int32, (rows, rows), 0) == lax.broadcasted_iota(
+        jnp.int32, (rows, rows), 1
+    )
+    ids = jnp.sum(
+        jnp.where(same, shift_ref[...].astype(jnp.float32), 0.0), axis=1, keepdims=True
+    ).astype(jnp.int32)
     step_y = (ids >= 3).astype(jnp.int32) + (ids >= 6).astype(jnp.int32)
     step_x = (ids - 3 * step_y - 1).astype(jnp.float32)
     step_y = (step_y - 1).astype(jnp.float32)
@@ -124,72 +130,60 @@
 
     pl.semaphore_wait(barrier, n_ptl - 1 + n_lib - 1)
 
-    def z_copy(i):
-        to = lax.rem(ptl + hop(i, n_ptl), n_ptl)
-        return pltpu.make_async_remote_copy(
-            src_ref=shifted.at[:, chunk(to)],
-            dst_ref=gath.at[i, lib],
-            send_sem=z_send.at[i - 1],
-            recv_sem=z_recv.at[i - 1],
+    def part(i, source, r):
+        return gath.at[i, source, pl.ds((r % pieces) * piece_rows, piece_rows)]
+
+    def z_copy(r):
+        to = lax.rem(ptl + r // pieces, n_ptl)
+        return pltpu.make_async_remote_copy(
+            src_ref=shifted.at[pl.ds((r % pieces) * piece_rows, piece_rows), chunk(to)],
+            dst_ref=part(r // pieces, lib, r),
+            send_sem=z_send.at[r - pieces],
+            recv_sem=z_recv.at[r - pieces],
             device_id={"ptl": to},
         )
 
-    run_loop(1, n_ptl, lambda i: z_copy(i).start())
+    for r in range(pieces, min(pieces + window, n_pieces)):
+        z_copy(r).start()
     own_copy = pltpu.make_async_copy(shifted.at[:, chunk(ptl)], gath.at[0, lib], own_sem)
     own_copy.start()
 
-    def x_copy(i, d):
-        return pltpu.make_async_remote_copy(
-            src_ref=gath.at[i, lib],
-            dst_ref=gath.at[i, lib],
-            send_sem=x_send.at[i, d - 1],
-            recv_sem=x_recv.at[i, d - 1],
-            device_id={"lib": lax.rem(x + d, n_x) * 2 + core},
-        )
-
-    def x_arrival(i, d):
-        source = lax.rem(x - d + n_x, n_x) * 2 + core
-        return pltpu.make_async_remote_copy(
-            src_ref=gath.at[i, source],
-            dst_ref=gath.at[i, source],
-            send_sem=x_send.at[i, d - 1],
-            recv_sem=x_recv.at[i, d - 1],
-            device_id={"lib": source},
-        )
-
-    def core_copy(i, d):
-        source = lax.rem(x - d + n_x, n_x) * 2 + core
-        return pltpu.make_async_remote_copy(
-            src_ref=gath.at[i, source],
-            dst_ref=gath.at[i, source],
-            send_sem=c_send.at[i, d],
-            recv_sem=c_recv.at[i, d],
-            device_id={"lib": mate},
-        )
-
-    def core_arrival(i, d):
-        source = lax.rem(x - d + n_x, n_x) * 2 + 1 - core
-        return pltpu.make_async_remote_copy(
-            src_ref=gath.at[i, source],
-            dst_ref=gath.at[i, source],
-            send_sem=c_send.at[i, d],
-            recv_sem=c_recv.at[i, d],
-            device_id={"lib": mate},
-        )
-
-    def z_arrival(i):
-        source = lax.rem(ptl - hop(i, n_ptl) + n_ptl, n_ptl)
-        return pltpu.make_async_remote_copy(
-            src_ref=shifted.at[:, chunk(ptl)],
-            dst_ref=gath.at[i, lib],
-            send_sem=z_send.at[i - 1],
-            recv_sem=z_recv.at[i - 1],
-            device_id={"ptl": source},
-        )
-
-    def spread(i):
-        run_loop(1, n_x, lambda d: x_copy(i, d).start())
-        core_copy(i, 0).start()
+    def x_source(d):
+        return lax.rem(x - d + n_x, n_x) * 2 + core
+
+    def lib_copy(r, d, source, send, recv, to):
+        return pltpu.make_async_remote_copy(
+            src_ref=part(r // pieces, source, r),
+            dst_ref=part(r // pieces, source, r),
+            send_sem=send.at[r, d],
+            recv_sem=recv.at[r, d],
+            device_id={"lib": to},
+        )
+
+    def x_copy(r, d):
+        return lib_copy(r, d - 1, lib, x_send, x_recv, lax.rem(x + d, n_x) * 2 + core)
+
+    def x_arrival(r, d):
+        return lib_copy(r, d - 1, x_source(d), x_send, x_recv, x_source(d))
+
+    def core_copy(r, d):
+        return lib_copy(r, d, x_source(d), c_send, c_recv, mate)
+
+    def core_arrival(r, d):
+        return lib_copy(r, d, x_source(d) + 1 - 2 * core, c_send, c_recv, mate)
+
+    def z_arrival(r):
+        return pltpu.make_async_remote_copy(
+            src_ref=part(r // pieces, lib, r),
+            dst_ref=part(r // pieces, lib, r),
+            send_sem=z_send.at[r - pieces],
+            recv_sem=z_recv.at[r - pieces],
+            device_id={"ptl": lax.rem(ptl - r // pieces + n_ptl, n_ptl)},
+        )
+
+    def spread(r):
+        run_loop(1, n_x, lambda d: x_copy(r, d).start())
+        core_copy(r, 0).start()
 
     def score_copy(i):
         return pltpu.make_async_remote_copy(
@@ -197,18 +191,19 @@
             dst_ref=srecv.at[i - 1],
             send_sem=s_send.at[i - 1],
             recv_sem=s_recv.at[i - 1],
-            device_id={"ptl": lax.rem(ptl - hop(i, n_ptl) + n_ptl, n_ptl)},
-        )
-
-    def relay(i):
+            device_id={"ptl": lax.rem(ptl - i + n_ptl, n_ptl)},
+        )
+
+    def relay(r):
         def forward(d):
-            x_arrival(i, d).wait_recv()
-            core_copy(i, d).start()
+            x_arrival(r, d).wait_recv()
+            core_copy(r, d).start()
 
         run_loop(1, n_x, forward)
-        run_loop(0, n_x, lambda d: core_arrival(i, d).wait_recv())
 
     def score(i):
+        for p in range(pieces):
+            run_loop(0, n_x, lambda d: core_arrival(i * pieces + p, d).wait_recv())
         block = gath[i].reshape(n_lib * rows, span)
         spart[i] = (
             lax.dot_general(
@@ -218,35 +213,48 @@
         )
 
     own_copy.wait()
-    spread(0)
+    for r in range(pieces):
+        spread(r)
+
+    noise2[:, 0:half] = noise_ref[...]
+    noise2[:, half:width] = noise_ref[...]
 
     ref_copy.wait()
     offset = ptl * part_cols - first_tile(ptl) * LANES
     place = lax.broadcasted_iota(jnp.int32, (1, span), 1)
     inside = (place >= offset) & (place < offset + part_cols)
-    noise = jnp.where(inside, noise_ref[:, chunk(ptl)], 0.0)
+    noise = jnp.where(inside, noise2[:, chunk(ptl)], 0.0)
     widened = refbuf[...].astype(jnp.float32)
     scaled = widened * noise
     weighted[...] = scaled.astype(jnp.bfloat16)
     half_norm = 0.5 * jnp.sum(widened * scaled, axis=1, keepdims=True)
 
-    def advance(i):
-        z_arrival(i).wait_recv()
-        spread(i)
-        relay(i - 1)
+    lag = min(2, pieces)
+    for r in range(pieces - lag):
+        relay(r)
+
+    def group(i):
+        for p in range(pieces):
+            r = i * pieces + p
+            z_arrival(r).wait_recv()
+            spread(r)
+
+            @pl.when(r + window < n_pieces)
+            def _():
+                z_copy(r + window).start()
+
+            relay(r - lag)
         score(i - 1)
 
-    z_arrival(1).wait_recv()
-    spread(1)
-    relay(0)
-    score(0)
+    group(1)
 
     def middle(i):
-        advance(i)
+        group(i)
         score_copy(i - 1).start()
 
     run_loop(2, n_ptl, middle)
-    relay(n_ptl - 1)
+    for r in range(n_pieces - lag, n_pieces):
+        relay(r)
     score(n_ptl - 1)
     score_copy(n_ptl - 1).start()
 
@@ -280,7 +288,10 @@
     for d in range(n_lib):
         total = total + stat_in[d, 1:2] * jnp.exp(stat_in[d, 0:1] - top)
     evidence = top + jnp.log(total)
-    evid_ref[...] = evidence
+    own_evidence = evidence[:, 0:rows]
+    for l in range(1, n_lib):
+        own_evidence = jnp.where(lib == l, evidence[:, l * rows : (l + 1) * rows], own_evidence)
+    evid_ref[...] = own_evidence
     own_post = jnp.exp(scores - evidence).astype(jnp.bfloat16)
     post[0] = own_post
 
@@ -290,16 +301,16 @@
             dst_ref=post.at[i],
             send_sem=p_send.at[i - 1],
             recv_sem=p_recv.at[i - 1],
-            device_id={"ptl": lax.rem(ptl + hop(i, n_ptl), n_ptl)},
+            device_id={"ptl": lax.rem(ptl + i, n_ptl)},
         )
 
     run_loop(1, n_ptl, lambda i: post_copy(i).start())
 
     onehot = (
-        class_ref[...] == lax.broadcasted_iota(jnp.int32, (class_ref.shape[0], CLASSES), 1)
+        class_ref[...] == lax.broadcasted_iota(jnp.int32, (CLASSES, class_ref.shape[1]), 0)
     ).astype(jnp.bfloat16)
     share_out[...] = lax.dot_general(
-        own_post, onehot, (((0,), (0,)), ((), ())), preferred_element_type=jnp.float32
+        own_post, onehot, (((0,), (1,)), ((), ())), preferred_element_type=jnp.float32
     ).reshape(n_lib, rows, CLASSES)
 
     def share_copy(d):
@@ -323,11 +334,18 @@
 
     lax.fori_loop(0, span // block, lambda b, c: (own_sums(b), c)[1], 0)
 
-    totbuf[...] = jnp.sum(own_post.astype(jnp.float32), axis=1, keepdims=True)
+    ones = jnp.ones((8, n_lib * rows), jnp.bfloat16)
+
+    def totals(weights):
+        return lax.dot_general(
+            ones, weights, (((1,), (1,)), ((), ())), preferred_element_type=jnp.float32
+        )
+
+    totbuf[...] = totals(own_post)
     run_loop(1, n_ptl, lambda i: post_copy(i).wait_recv())
 
     def add_total(i):
-        totbuf[...] += jnp.sum(post[i].astype(jnp.float32), axis=1, keepdims=True)
+        totbuf[...] += totals(post[i])
 
     run_loop(1, n_ptl, add_total)
 
@@ -341,8 +359,11 @@
 
     lax.fori_loop(0, span // block, lambda b, c: (other_sums(b), c)[1], 0)
 
-    own_total = total_ref.shape[0]
-    total_ref[...] = totbuf[pl.ds(pl.multiple_of(ptl * own_total, 8), own_total), :]
+    count = total_ref.shape[1]
+    own_total = totbuf[0:1, 0:count]
+    for z in range(1, n_ptl):
+        own_total = jnp.where(ptl == z, totbuf[0:1, z * count : (z + 1) * count], own_total)
+    total_ref[...] = own_total
 
     share = share_out[lib]
     for d in range(1, n_lib):
@@ -351,7 +372,6 @@
     share_ref[...] = share
 
     def ptl_sent(i):
-        z_copy(i).wait_send()
         score_copy(i).wait_send()
         post_copy(i).wait_send()
 
@@ -359,13 +379,26 @@
         stat_copy(d).wait_send()
         share_copy(d).wait_send()
 
-    def spread_sent(i):
-        run_loop(1, n_x, lambda d: x_copy(i, d).wait_send())
-        run_loop(0, n_x, lambda d: core_copy(i, d).wait_send())
+    def spread_sent(r):
+        run_loop(1, n_x, lambda d: x_copy(r, d).wait_send())
+        run_loop(0, n_x, lambda d: core_copy(r, d).wait_send())
 
     run_loop(1, n_ptl, ptl_sent)
     run_loop(1, n_lib, lib_sent)
-    run_loop(0, n_ptl, spread_sent)
+    run_loop(pieces, n_pieces, lambda r: z_copy(r).wait_send())
+    run_loop(0, n_pieces, spread_sent)
+
+
+def finish(n_ptl, part_cols, sums_in, evid_in, share_in, total_in, sums, evid, share, total):
+    span = sums_in.shape[1]
+    z = lax.axis_index("ptl")
+    tiles = n_ptl * part_cols // LANES
+    offset = z * part_cols - jnp.minimum((z * part_cols) // LANES, tiles - span // LANES) * LANES
+    turned = pltpu.roll(sums_in[...], lax.rem(span - offset, span), 1)
+    sums[...] = turned[:, 0:part_cols]
+    evid[...] = evid_in[...]
+    share[...] = share_in[...]
+    total[...] = total_in[...]
 
 
 def trig_table(half):
@@ -388,19 +421,23 @@
     n_x = n_lib // 2
     group = n_lib * rows
     own_total = projections // n_ptl
+    pieces = 3 if rows % 48 == 0 else 1
+    window = WINDOW
+    n_pieces = n_ptl * pieces
     vmem = pl.BlockSpec(memory_space=pltpu.VMEM)
     dma = pltpu.SemaphoreType.DMA
     sums, evidence, share, total = pl.pallas_call(
-        functools.partial(kernel, n_lib, n_ptl, span),
+        functools.partial(kernel, n_lib, n_ptl, span, pieces, window),
         out_shape=(
             jax.ShapeDtypeStruct((projections, span), jnp.float32),
-            jax.ShapeDtypeStruct((1, group), jnp.float32),
+            jax.ShapeDtypeStruct((1, rows), jnp.float32),
             jax.ShapeDtypeStruct((rows, CLASSES), jnp.float32),
-            jax.ShapeDtypeStruct((own_total, 1), jnp.float32),
+            jax.ShapeDtypeStruct((1, own_total), jnp.float32),
         ),
         in_specs=[vmem, vmem, vmem, pl.BlockSpec(memory_space=pl.ANY), vmem, vmem],
         out_specs=(vmem, vmem, vmem, vmem),
         scratch_shapes=[
+            pltpu.VMEM((1, width), jnp.float32),
             pltpu.VMEM((rows, width), jnp.bfloat16),
             pltpu.VMEM((n_ptl, n_lib, rows, span), jnp.bfloat16),
             pltpu.VMEM((projections, span), jnp.bfloat16),
@@ -412,15 +449,15 @@
             pltpu.VMEM((n_lib, 8, group), jnp.float32),
             pltpu.VMEM((n_lib, rows, CLASSES), jnp.float32),
             pltpu.VMEM((n_lib - 1, rows, CLASSES), jnp.float32),
-            pltpu.VMEM((projections, 1), jnp.float32),
+            pltpu.VMEM((8, projections), jnp.float32),
             dma,
             dma,
-            dma((n_ptl - 1,)),
-            dma((n_ptl - 1,)),
-            dma((n_ptl, n_x - 1)),
-            dma((n_ptl, n_x - 1)),
-            dma((n_ptl, n_x)),
-            dma((n_ptl, n_x)),
+            dma((n_pieces - pieces,)),
+            dma((n_pieces - pieces,)),
+            dma((n_pieces, n_x - 1)),
+            dma((n_pieces, n_x - 1)),
+            dma((n_pieces, n_x)),
+            dma((n_pieces, n_x)),
             dma((n_ptl - 1,)),
             dma((n_ptl - 1,)),
             dma((n_lib - 1,)),
@@ -435,17 +472,31 @@
         ),
     )(
         particles,
-        shifts[:, None],
+        shifts[None, :],
         trig_table(width // 2),
         references,
-        jnp.concatenate([inv_noise, inv_noise])[None, :],
-        proj_class[:, None],
+        inv_noise[None, :],
+        proj_class[None, :],
     )
-    ptl, lib = lax.axis_index("ptl"), lax.axis_index("lib")
-    first = jnp.minimum((ptl * part_cols) // LANES, tiles - span // LANES) * LANES
-    out_sums = lax.dynamic_slice_in_dim(sums, ptl * part_cols - first, part_cols, 1)
-    own_evidence = lax.dynamic_slice_in_dim(evidence[0], lib * rows, rows, 0)
-    return own_evidence, share, out_sums, total[:, 0]
+    block = projections // 4
+
+    def fixed(shape):
+        return pl.BlockSpec(shape, lambda i: (0, 0))
+
+    small = [fixed((1, rows)), fixed((rows, CLASSES)), fixed((1, own_total))]
+    sums, evidence, share, total = pl.pallas_call(
+        functools.partial(finish, n_ptl, part_cols),
+        grid=(4,),
+        out_shape=(
+            jax.ShapeDtypeStruct((projections, part_cols), jnp.float32),
+            jax.ShapeDtypeStruct((1, rows), jnp.float32),
+            jax.ShapeDtypeStruct((rows, CLASSES), jnp.float32),
+            jax.ShapeDtypeStruct((1, own_total), jnp.float32),
+        ),
+        in_specs=[pl.BlockSpec((block, span), lambda i: (i, 0))] + small,
+        out_specs=tuple([pl.BlockSpec((block, part_cols), lambda i: (i, 0))] + small),
+    )(sums, evidence, share, total)
+    return evidence[0], share, sums, total[0]
 
 
 def solution(mesh):

time: 72.7 us -> 66.9 us (0.920)
  the two profiles are of different devices: /device:TPU:18 before, /device:TPU:30 now
where the time goes in v2:
time: 66.9 us; the launch traced here: 66.5 us
  Pallas kernels  60.4 us (90%)
  local copies, waits for them, and re-layouts  5.52 us (8%)
    pallas_call x1, Pallas kernels, on_device(): pl.pallas_call(functools.partial(kernel, n_lib, n_ptl, span, pieces, wind...  56.5 us
    unnamed x2, local copies, waits for them, and re-layouts  4.17 us
    pallas_call x1, Pallas kernels, on_device(): pl.pallas_call(functools.partial(finish, n_ptl, part_cols), grid=(4,), ou...  3.88 us
    broadcast_in_dim x1, local copies, waits for them, and re-layouts, on_device(): inv_noise[None, :]  1.35 us

profile of v2, /device:TPU:30, one launch (start us, length us, event | category | flops | bytes accessed | tf_op | source)
XLA Modules:
  0.0 66.5 jit_solution(9543846923906376189)
XLA Ops:
  0.6 1.3 %broadcast_in_dim.10.noise_ref = f32[1,4992]{1,0:T(1,128)} reshape(f32[4992]{0:T(1024)} %param.9) | data formatting | bytes 39936 | tf_op jit(solution)/shard_map/broadcast_in_dim | solution.py:478
  2.0 56.5 %shard_map.93 = (f32[128,2560]{1,0:T(8,128)}, f32[1,48]{1,0:T(1,128)}, f32[48,16]{1,0:T(8,128)}, f32[1,32]{1,0:T(1,128)}) custom-call(bf16[48,9984]{1,0:T(8,128)(2,1)} %part_ref.1, s32[1,48]{1,0:T(1,128)} %bitcast.4, f32[8,4992]{1,0:T(8,128)} %constant.2.clone.table_ref, bf16[128,9984]{1,0:T(8,128)(2,1)} %refs_hbm.1, f32[1,4992]{1,0:T(1,128)} %broadcast_in_dim.10.noise_ref, ...), custom_call_target="tpu_custom_call" | custom-call | tf_op jit(solution)/shard_map/pallas_call | solution.py:429
  58.5 3.9 %shard_map.94 = (f32[128,2496]{1,0:T(8,128)}, f32[1,48]{1,0:T(1,128)}, f32[48,16]{1,0:T(8,128)}, f32[1,32]{1,0:T(1,128)}) custom-call(f32[128,2560]{1,0:T(8,128)} %get-tuple-element.12.sums_in, f32[1,48]{1,0:T(1,128)} %get-tuple-element.13.evid_in, f32[48,16]{1,0:T(8,128)} %get-tuple-element.14.share_in, f32[1,32]{1,0:T(1,128)} %get-tuple-element.15.total_in), custom_call_target="tpu_custom_call" | custom-call | tf_op jit(solution)/shard_map/pallas_call | solution.py:487
  62.4 1.4 %copy.10 = f32[48,16]{0,1:T(8,128)} copy(f32[48,16]{1,0:T(8,128)} %get-tuple-element.21) | data formatting | bytes 6144
  63.8 2.8 %copy.11 = f32[128,2496]{0,1:T(8,128)} copy(f32[128,2496]{1,0:T(8,128)} %get-tuple-element.22) | data formatting | bytes 2555904

commit v3 on v2

--- a/solution.py
+++ b/solution.py
@@ -25,6 +25,19 @@
             return carry
 
         lax.fori_loop(low, high, step, 0)
+
+
+def diagonal(count):
+    shape = (count, count)
+    return lax.broadcasted_iota(jnp.int32, shape, 0) == lax.broadcasted_iota(jnp.int32, shape, 1)
+
+
+def to_column(row):
+    return jnp.sum(jnp.where(diagonal(row.shape[1]), row, 0.0), axis=1, keepdims=True)
+
+
+def to_row(column):
+    return jnp.sum(jnp.where(diagonal(column.shape[0]), column, 0.0), axis=0, keepdims=True)
 
 
 def kernel(
@@ -56,6 +69,7 @@
     share_out,
     share_in,
     totbuf,
+    own_part,
     ref_sem,
     own_sem,
     z_send,
@@ -105,12 +119,7 @@
     ref_copy = pltpu.make_async_copy(refs_hbm.at[:, chunk(ptl)], refbuf, ref_sem)
     ref_copy.start()
 
-    same = lax.broadcasted_iota(jnp.int32, (rows, rows), 0) == lax.broadcasted_iota(
-        jnp.int32, (rows, rows), 1
-    )
-    ids = jnp.sum(
-        jnp.where(same, shift_ref[...].astype(jnp.float32), 0.0), axis=1, keepdims=True
-    ).astype(jnp.int32)
+    ids = to_column(shift_ref[...].astype(jnp.float32)).astype(jnp.int32)
     step_y = (ids >= 3).astype(jnp.int32) + (ids >= 6).astype(jnp.int32)
     step_x = (ids - 3 * step_y - 1).astype(jnp.float32)
     step_y = (step_y - 1).astype(jnp.float32)
@@ -207,7 +216,7 @@
         block = gath[i].reshape(n_lib * rows, span)
         spart[i] = (
             lax.dot_general(
-                weighted[...], block, (((1,), (1,)), ((), ())), preferred_element_type=jnp.float32
+                block, weighted[...], (((1,), (1,)), ((), ())), preferred_element_type=jnp.float32
             )
             - half_norm
         )
@@ -227,7 +236,7 @@
     widened = refbuf[...].astype(jnp.float32)
     scaled = widened * noise
     weighted[...] = scaled.astype(jnp.bfloat16)
-    half_norm = 0.5 * jnp.sum(widened * scaled, axis=1, keepdims=True)
+    half_norm = to_row(0.5 * jnp.sum(widened * scaled, axis=1, keepdims=True))
 
     lag = min(2, pieces)
     for r in range(pieces - lag):
@@ -265,9 +274,10 @@
     run_loop(1, n_ptl, add_scores)
     scores = spart[0]
 
-    peak = jnp.max(scores, axis=0, keepdims=True)
+    own_peak = jnp.max(scores, axis=1, keepdims=True)
+    peak = to_row(own_peak)
     stat[0:1] = peak
-    stat[1:2] = jnp.sum(jnp.exp(scores - peak), axis=0, keepdims=True)
+    stat[1:2] = to_row(jnp.sum(jnp.exp(scores - own_peak), axis=1, keepdims=True))
 
     def stat_copy(d):
         return pltpu.make_async_remote_copy(
@@ -292,7 +302,7 @@
     for l in range(1, n_lib):
         own_evidence = jnp.where(lib == l, evidence[:, l * rows : (l + 1) * rows], own_evidence)
     evid_ref[...] = own_evidence
-    own_post = jnp.exp(scores - evidence).astype(jnp.bfloat16)
+    own_post = jnp.exp(scores - to_column(evidence)).astype(jnp.bfloat16)
     post[0] = own_post
 
     def post_copy(i):
@@ -309,9 +319,11 @@
     onehot = (
         class_ref[...] == lax.broadcasted_iota(jnp.int32, (CLASSES, class_ref.shape[1]), 0)
     ).astype(jnp.bfloat16)
-    share_out[...] = lax.dot_general(
-        own_post, onehot, (((0,), (1,)), ((), ())), preferred_element_type=jnp.float32
-    ).reshape(n_lib, rows, CLASSES)
+    shares = lax.dot_general(
+        onehot, own_post, (((1,), (1,)), ((), ())), preferred_element_type=jnp.float32
+    )
+    for l in range(n_lib):
+        share_out[l] = shares[:, l * rows : (l + 1) * rows]
 
     def share_copy(d):
         to = lax.rem(lib + d, n_lib)
@@ -325,12 +337,17 @@
 
     run_loop(1, n_lib, lambda d: share_copy(d).start())
 
+    def weigh(weights, images):
+        return lax.dot_general(
+            weights, images, (((0,), (0,)), ((), ())), preferred_element_type=jnp.float32
+        )
+
     block = 512 if span % 512 == 0 else LANES
 
     def own_sums(b):
         cols = pl.ds(pl.multiple_of(b * block, block), block)
         images = gath[0, :, :, cols].reshape(n_lib * rows, block)
-        sums_ref[:, cols] = jnp.dot(own_post, images, preferred_element_type=jnp.float32)
+        own_part[:, cols] = weigh(own_post, images)
 
     lax.fori_loop(0, span // block, lambda b, c: (own_sums(b), c)[1], 0)
 
@@ -338,7 +355,7 @@
 
     def totals(weights):
         return lax.dot_general(
-            ones, weights, (((1,), (1,)), ((), ())), preferred_element_type=jnp.float32
+            ones, weights, (((1,), (0,)), ((), ())), preferred_element_type=jnp.float32
         )
 
     totbuf[...] = totals(own_post)
@@ -351,11 +368,11 @@
 
     def other_sums(b):
         cols = pl.ds(pl.multiple_of(b * block, block), block)
-        sums = sums_ref[:, cols]
+        sums = own_part[:, cols]
         for i in range(1, n_ptl):
             images = gath[i, :, :, cols].reshape(n_lib * rows, block)
-            sums = sums + jnp.dot(post[i], images, preferred_element_type=jnp.float32)
-        sums_ref[:, cols] = sums
+            sums = sums + weigh(post[i], images)
+        sums_ref[cols, :] = sums.T
 
     lax.fori_loop(0, span // block, lambda b, c: (other_sums(b), c)[1], 0)
 
@@ -389,16 +406,20 @@
     run_loop(0, n_pieces, spread_sent)
 
 
-def finish(n_ptl, part_cols, sums_in, evid_in, share_in, total_in, sums, evid, share, total):
-    span = sums_in.shape[1]
+def finish(n_ptl, sums_in, evid_in, share_in, total_in, sums, evid, share, total, sem):
+    part_cols = sums.shape[0]
+    span = sums_in.shape[0]
     z = lax.axis_index("ptl")
     tiles = n_ptl * part_cols // LANES
     offset = z * part_cols - jnp.minimum((z * part_cols) // LANES, tiles - span // LANES) * LANES
-    turned = pltpu.roll(sums_in[...], lax.rem(span - offset, span), 1)
-    sums[...] = turned[:, 0:part_cols]
+    copy = pltpu.make_async_copy(
+        sums_in.at[pl.ds(pl.multiple_of(offset, 8), part_cols)], sums, sem
+    )
+    copy.start()
     evid[...] = evid_in[...]
     share[...] = share_in[...]
     total[...] = total_in[...]
+    copy.wait()
 
 
 def trig_table(half):
@@ -429,9 +450,9 @@
     sums, evidence, share, total = pl.pallas_call(
         functools.partial(kernel, n_lib, n_ptl, span, pieces, window),
         out_shape=(
-            jax.ShapeDtypeStruct((projections, span), jnp.float32),
+            jax.ShapeDtypeStruct((span, projections), jnp.float32),
             jax.ShapeDtypeStruct((1, rows), jnp.float32),
-            jax.ShapeDtypeStruct((rows, CLASSES), jnp.float32),
+            jax.ShapeDtypeStruct((CLASSES, rows), jnp.float32),
             jax.ShapeDtypeStruct((1, own_total), jnp.float32),
         ),
         in_specs=[vmem, vmem, vmem, pl.BlockSpec(memory_space=pl.ANY), vmem, vmem],
@@ -442,14 +463,15 @@
             pltpu.VMEM((n_ptl, n_lib, rows, span), jnp.bfloat16),
             pltpu.VMEM((projections, span), jnp.bfloat16),
             pltpu.VMEM((projections, span), jnp.bfloat16),
-            pltpu.VMEM((n_ptl, projections, group), jnp.float32),
-            pltpu.VMEM((n_ptl - 1, projections, group), jnp.float32),
-            pltpu.VMEM((n_ptl, projections, group), jnp.bfloat16),
+            pltpu.VMEM((n_ptl, group, projections), jnp.float32),
+            pltpu.VMEM((n_ptl - 1, group, projections), jnp.float32),
+            pltpu.VMEM((n_ptl, group, projections), jnp.bfloat16),
             pltpu.VMEM((8, group), jnp.float32),
             pltpu.VMEM((n_lib, 8, group), jnp.float32),
-            pltpu.VMEM((n_lib, rows, CLASSES), jnp.float32),
-            pltpu.VMEM((n_lib - 1, rows, CLASSES), jnp.float32),
+            pltpu.VMEM((n_lib, CLASSES, rows), jnp.float32),
+            pltpu.VMEM((n_lib - 1, CLASSES, rows), jnp.float32),
             pltpu.VMEM((8, projections), jnp.float32),
+            pltpu.VMEM((projections, span), jnp.float32),
             dma,
             dma,
             dma((n_pieces - pieces,)),
@@ -478,25 +500,20 @@
         inv_noise[None, :],
         proj_class[None, :],
     )
-    block = projections // 4
-
-    def fixed(shape):
-        return pl.BlockSpec(shape, lambda i: (0, 0))
-
-    small = [fixed((1, rows)), fixed((rows, CLASSES)), fixed((1, own_total))]
+    far = pl.BlockSpec(memory_space=pl.ANY)
     sums, evidence, share, total = pl.pallas_call(
-        functools.partial(finish, n_ptl, part_cols),
-        grid=(4,),
+        functools.partial(finish, n_ptl),
         out_shape=(
-            jax.ShapeDtypeStruct((projections, part_cols), jnp.float32),
+            jax.ShapeDtypeStruct((part_cols, projections), jnp.float32),
             jax.ShapeDtypeStruct((1, rows), jnp.float32),
-            jax.ShapeDtypeStruct((rows, CLASSES), jnp.float32),
+            jax.ShapeDtypeStruct((CLASSES, rows), jnp.float32),
             jax.ShapeDtypeStruct((1, own_total), jnp.float32),
         ),
-        in_specs=[pl.BlockSpec((block, span), lambda i: (i, 0))] + small,
-        out_specs=tuple([pl.BlockSpec((block, part_cols), lambda i: (i, 0))] + small),
+        in_specs=[far, vmem, vmem, vmem],
+        out_specs=(far, vmem, vmem, vmem),
+        scratch_shapes=[dma],
     )(sums, evidence, share, total)
-    return evidence[0], share, sums, total[0]
+    return evidence[0], share.T, sums.T, total[0]
 
 
 def solution(mesh):

time: 66.9 us -> 98 us (1.46)
  the two profiles are of different devices: /device:TPU:30 before, /device:TPU:0 now
where the time goes in v3:
time: 98 us; the launch traced here: 96.7 us
  Pallas kernels  94.8 us (97%)
  local copies, waits for them, and re-layouts  1.35 us (1%)
    pallas_call x1, Pallas kernels, on_device(): pl.pallas_call(functools.partial(kernel, n_lib, n_ptl, span, pieces, wind...  53.6 us
    pallas_call x1, Pallas kernels, on_device(): pl.pallas_call(functools.partial(finish, n_ptl), out_shape=(jax.ShapeDtyp...  41.1 us

profile of v3, /device:TPU:0, one launch (start us, length us, event | category | flops | bytes accessed | tf_op | source)
XLA Modules:
  0.0 96.7 jit_solution(2211530144189494642)
XLA Ops:
  0.6 1.3 %broadcast_in_dim.10.noise_ref = f32[1,4992]{1,0:T(1,128)} reshape(f32[4992]{0:T(1024)} %param.9) | data formatting | bytes 39936 | tf_op jit(solution)/shard_map/broadcast_in_dim | solution.py:500
  2.0 53.6 %shard_map.93 = (f32[2560,128]{1,0:T(8,128)}, f32[1,48]{1,0:T(1,128)}, f32[16,48]{1,0:T(8,128)}, f32[1,32]{1,0:T(1,128)}) custom-call(bf16[48,9984]{1,0:T(8,128)(2,1)} %part_ref.1, s32[1,48]{1,0:T(1,128)} %bitcast.6, f32[8,4992]{1,0:T(8,128)} %constant.2.clone.table_ref, bf16[128,9984]{1,0:T(8,128)(2,1)} %refs_hbm.1, f32[1,4992]{1,0:T(1,128)} %broadcast_in_dim.10.noise_ref, ...), custom_call_target="tpu_custom_call" | custom-call | tf_op jit(solution)/shard_map/pallas_call | solution.py:450
  55.6 41.1 %shard_map.94 = (f32[2496,128]{1,0:T(8,128)}, f32[1,48]{1,0:T(1,128)}, f32[16,48]{1,0:T(8,128)}, f32[1,32]{1,0:T(1,128)}) custom-call(f32[2560,128]{1,0:T(8,128)} %get-tuple-element.12.sums_in, f32[1,48]{1,0:T(1,128)} %get-tuple-element.13.evid_in, f32[16,48]{1,0:T(8,128)} %get-tuple-element.14.share_in, f32[1,32]{1,0:T(1,128)} %get-tuple-element.15.total_in), custom_call_target="tpu_custom_call" | custom-call | tf_op jit(solution)/shard_map/pallas_call | solution.py:504

commit v4 on v3

--- a/solution.py
+++ b/solution.py
@@ -25,6 +25,11 @@
             return carry
 
         lax.fori_loop(low, high, step, 0)
+
+
+def hop(index, count):
+    odd = index % 2
+    return odd * ((index + 1) // 2) + (1 - odd) * (count - index // 2)
 
 
 def diagonal(count):
@@ -143,7 +148,7 @@
         return gath.at[i, source, pl.ds((r % pieces) * piece_rows, piece_rows)]
 
     def z_copy(r):
-        to = lax.rem(ptl + r // pieces, n_ptl)
+        to = lax.rem(ptl + hop(r // pieces, n_ptl), n_ptl)
         return pltpu.make_async_remote_copy(
             src_ref=shifted.at[pl.ds((r % pieces) * piece_rows, piece_rows), chunk(to)],
             dst_ref=part(r // pieces, lib, r),
@@ -187,7 +192,7 @@
             dst_ref=part(r // pieces, lib, r),
             send_sem=z_send.at[r - pieces],
             recv_sem=z_recv.at[r - pieces],
-            device_id={"ptl": lax.rem(ptl - r // pieces + n_ptl, n_ptl)},
+            device_id={"ptl": lax.rem(ptl - hop(r // pieces, n_ptl) + n_ptl, n_ptl)},
         )
 
     def spread(r):
@@ -200,7 +205,7 @@
             dst_ref=srecv.at[i - 1],
             send_sem=s_send.at[i - 1],
             recv_sem=s_recv.at[i - 1],
-            device_id={"ptl": lax.rem(ptl - i + n_ptl, n_ptl)},
+            device_id={"ptl": lax.rem(ptl - hop(i, n_ptl) + n_ptl, n_ptl)},
         )
 
     def relay(r):
@@ -311,7 +316,7 @@
             dst_ref=post.at[i],
             send_sem=p_send.at[i - 1],
             recv_sem=p_recv.at[i - 1],
-            device_id={"ptl": lax.rem(ptl + i, n_ptl)},
+            device_id={"ptl": lax.rem(ptl + hop(i, n_ptl), n_ptl)},
         )
 
     run_loop(1, n_ptl, lambda i: post_copy(i).start())
@@ -509,7 +514,7 @@
             jax.ShapeDtypeStruct((CLASSES, rows), jnp.float32),
             jax.ShapeDtypeStruct((1, own_total), jnp.float32),
         ),
-        in_specs=[far, vmem, vmem, vmem],
+        in_specs=[vmem, vmem, vmem, vmem],
         out_specs=(far, vmem, vmem, vmem),
         scratch_shapes=[dma],
     )(sums, evidence, share, total)

time: 98 us -> 58.1 us (0.59); the launches traced: 96.7 us -> 57.8 us
  Pallas kernels: 94.8 us -> 55.8 us
    pallas_call x1, Pallas kernels: 41.1 us -> 2.98 us  [on_device(): pl.pallas_call(functools.partial(finish, n_ptl), out_shape=(jax.ShapeDtyp...]
where the time goes in v4:
time: 58.1 us; the launch traced here: 57.8 us
  Pallas kernels  55.8 us (96%)
  local copies, waits for them, and re-layouts  1.35 us (2%)
  between operations  0.64 us (1%)
    pallas_call x1, Pallas kernels, on_device(): pl.pallas_call(functools.partial(kernel, n_lib, n_ptl, span, pieces, wind...  52.9 us
    pallas_call x1, Pallas kernels, on_device(): pl.pallas_call(functools.partial(finish, n_ptl), out_shape=(jax.ShapeDtyp...  2.98 us
    broadcast_in_dim x1, local copies, waits for them, and re-layouts, on_device(): inv_noise[None, :]  1.35 us

profile of v4, /device:TPU:0, one launch (start us, length us, event | category | flops | bytes accessed | tf_op | source)
XLA Modules:
  0.0 57.8 jit_solution(14549369474726427927)
XLA Ops:
  0.6 1.3 %broadcast_in_dim.10.noise_ref = f32[1,4992]{1,0:T(1,128)} reshape(f32[4992]{0:T(1024)} %param.9) | data formatting | bytes 39936 | tf_op jit(solution)/shard_map/broadcast_in_dim | solution.py:505
  2.0 52.9 %shard_map.93 = (f32[2560,128]{1,0:T(8,128)}, f32[1,48]{1,0:T(1,128)}, f32[16,48]{1,0:T(8,128)}, f32[1,32]{1,0:T(1,128)}) custom-call(bf16[48,9984]{1,0:T(8,128)(2,1)} %part_ref.1, s32[1,48]{1,0:T(1,128)} %bitcast.6, f32[8,4992]{1,0:T(8,128)} %constant.2.clone.table_ref, bf16[128,9984]{1,0:T(8,128)(2,1)} %refs_hbm.1, f32[1,4992]{1,0:T(1,128)} %broadcast_in_dim.10.noise_ref, ...), custom_call_target="tpu_custom_call" | custom-call | tf_op jit(solution)/shard_map/pallas_call | solution.py:455
  54.9 3.0 %shard_map.94 = (f32[2496,128]{1,0:T(8,128)}, f32[1,48]{1,0:T(1,128)}, f32[16,48]{1,0:T(8,128)}, f32[1,32]{1,0:T(1,128)}) custom-call(f32[2560,128]{1,0:T(8,128)} %get-tuple-element.12.sums_in, f32[1,48]{1,0:T(1,128)} %get-tuple-element.13.evid_in, f32[16,48]{1,0:T(8,128)} %get-tuple-element.14.share_in, f32[1,32]{1,0:T(1,128)} %get-tuple-element.15.total_in), custom_call_target="tpu_custom_call" | custom-call | tf_op jit(solution)/shard_map/pallas_call | solution.py:509

commit v5 on v4

--- a/solution.py
+++ b/solution.py
@@ -10,7 +10,7 @@
 from jax.sharding import PartitionSpec as P
 
 CLASSES = 16
-WINDOW = 3
+WINDOW = 4
 LANES = 128
 
 
@@ -51,7 +51,7 @@
     span,
     pieces,
     window,
-    part_ref,
+    part_hbm,
     shift_ref,
     table_ref,
     refs_hbm,
@@ -62,6 +62,7 @@
     share_ref,
     total_ref,
     noise2,
+    part_ref,
     shifted,
     gath,
     refbuf,
@@ -75,6 +76,7 @@
     share_in,
     totbuf,
     own_part,
+    part_sem,
     ref_sem,
     own_sem,
     z_send,
@@ -110,6 +112,8 @@
     def chunk(z):
         return pl.ds(pl.multiple_of(first_tile(z) * LANES, LANES), span)
 
+    part_copy = pltpu.make_async_copy(part_hbm, part_ref, part_sem)
+    part_copy.start()
     barrier = pltpu.get_barrier_semaphore()
 
     def greet_ptl(step):
@@ -130,6 +134,7 @@
     step_y = (step_y - 1).astype(jnp.float32)
     cos_x = jnp.where(step_x == 0.0, 1.0, table_ref[0:1, 0:LANES])
     sin_x = step_x * table_ref[1:2, 0:LANES]
+    part_copy.wait()
     for tile in range(half // LANES):
         lo = slice(tile * LANES, (tile + 1) * LANES)
         hi = slice(half + tile * LANES, half + (tile + 1) * LANES)
@@ -230,8 +235,10 @@
     for r in range(pieces):
         spread(r)
 
-    noise2[:, 0:half] = noise_ref[...]
-    noise2[:, half:width] = noise_ref[...]
+    for tile in range(half // LANES):
+        row = noise_ref[tile : tile + 1, :]
+        noise2[:, tile * LANES : (tile + 1) * LANES] = row
+        noise2[:, half + tile * LANES : half + (tile + 1) * LANES] = row
 
     ref_copy.wait()
     offset = ptl * part_cols - first_tile(ptl) * LANES
@@ -411,20 +418,36 @@
     run_loop(0, n_pieces, spread_sent)
 
 
-def finish(n_ptl, sums_in, evid_in, share_in, total_in, sums, evid, share, total, sem):
+def finish(
+    n_ptl, sums_in, evid_in, share_in, total_in, sums, evid, share, total, buffer, read_sem, write_sem
+):
     part_cols = sums.shape[0]
     span = sums_in.shape[0]
     z = lax.axis_index("ptl")
     tiles = n_ptl * part_cols // LANES
     offset = z * part_cols - jnp.minimum((z * part_cols) // LANES, tiles - span // LANES) * LANES
-    copy = pltpu.make_async_copy(
-        sums_in.at[pl.ds(pl.multiple_of(offset, 8), part_cols)], sums, sem
-    )
-    copy.start()
+    chunks = buffer.shape[0]
+    step = part_cols // chunks
+
+    def read(c):
+        rows = pl.ds(pl.multiple_of(offset + c * step, 8), step)
+        return pltpu.make_async_copy(sums_in.at[rows], buffer.at[c], read_sem.at[c])
+
+    def write(c):
+        return pltpu.make_async_copy(
+            buffer.at[c], sums.at[pl.ds(c * step, step)], write_sem.at[c]
+        )
+
+    for c in range(chunks):
+        read(c).start()
     evid[...] = evid_in[...]
     share[...] = share_in[...]
     total[...] = total_in[...]
-    copy.wait()
+    for c in range(chunks):
+        read(c).wait()
+        write(c).start()
+    for c in range(chunks):
+        write(c).wait()
 
 
 def trig_table(half):
@@ -451,6 +474,7 @@
     window = WINDOW
     n_pieces = n_ptl * pieces
     vmem = pl.BlockSpec(memory_space=pltpu.VMEM)
+    far = pl.BlockSpec(memory_space=pl.ANY)
     dma = pltpu.SemaphoreType.DMA
     sums, evidence, share, total = pl.pallas_call(
         functools.partial(kernel, n_lib, n_ptl, span, pieces, window),
@@ -460,10 +484,11 @@
             jax.ShapeDtypeStruct((CLASSES, rows), jnp.float32),
             jax.ShapeDtypeStruct((1, own_total), jnp.float32),
         ),
-        in_specs=[vmem, vmem, vmem, pl.BlockSpec(memory_space=pl.ANY), vmem, vmem],
+        in_specs=[far, vmem, vmem, far, vmem, vmem],
         out_specs=(vmem, vmem, vmem, vmem),
         scratch_shapes=[
             pltpu.VMEM((1, width), jnp.float32),
+            pltpu.VMEM((rows, width), jnp.bfloat16),
             pltpu.VMEM((rows, width), jnp.bfloat16),
             pltpu.VMEM((n_ptl, n_lib, rows, span), jnp.bfloat16),
             pltpu.VMEM((projections, span), jnp.bfloat16),
@@ -477,6 +502,7 @@
             pltpu.VMEM((n_lib - 1, CLASSES, rows), jnp.float32),
             pltpu.VMEM((8, projections), jnp.float32),
             pltpu.VMEM((projections, span), jnp.float32),
+            dma,
             dma,
             dma,
             dma((n_pieces - pieces,)),
@@ -502,10 +528,10 @@
         shifts[None, :],
         trig_table(width // 2),
         references,
-        inv_noise[None, :],
+        inv_noise.reshape(-1, LANES),
         proj_class[None, :],
     )
-    far = pl.BlockSpec(memory_space=pl.ANY)
+    chunks = next(c for c in (6, 4, 3, 2, 1) if part_cols % (8 * c) == 0)
     sums, evidence, share, total = pl.pallas_call(
         functools.partial(finish, n_ptl),
         out_shape=(
@@ -514,9 +540,13 @@
             jax.ShapeDtypeStruct((CLASSES, rows), jnp.float32),
             jax.ShapeDtypeStruct((1, own_total), jnp.float32),
         ),
-        in_specs=[vmem, vmem, vmem, vmem],
+        in_specs=[far, vmem, vmem, vmem],
         out_specs=(far, vmem, vmem, vmem),
-        scratch_shapes=[dma],
+        scratch_shapes=[
+            pltpu.VMEM((chunks, part_cols // chunks, projections), jnp.float32),
+            dma((chunks,)),
+            dma((chunks,)),
+        ],
     )(sums, evidence, share, total)
     return evidence[0], share.T, sums.T, total[0]
 

time: 58.1 us -> 56.7 us (0.976)
  local copies, waits for them, and re-layouts: 1.35 us -> 0 us
    broadcast_in_dim x1 -> x0, local copies, waits for them, and re-layouts: 1.35 us -> none  [on_device(): inv_noise[None, :]]
where the time goes in v5:
time: 56.7 us; the launch traced here: 56.5 us
  Pallas kernels  55.8 us (98%)
  between operations  0.64 us (1%)
    pallas_call x1, Pallas kernels, on_device(): pl.pallas_call(functools.partial(kernel, n_lib, n_ptl, span, pieces, wind...  52.4 us
    pallas_call x1, Pallas kernels, on_device(): pl.pallas_call(functools.partial(finish, n_ptl), out_shape=(jax.ShapeDtyp...  3.47 us

profile of v5, /device:TPU:0, one launch (start us, length us, event | category | flops | bytes accessed | tf_op | source)
XLA Modules:
  0.0 56.5 jit_solution(12133437515079430379)
XLA Ops:
  0.6 52.4 %shard_map.93 = (f32[2560,128]{1,0:T(8,128)}, f32[1,48]{1,0:T(1,128)}, f32[16,48]{1,0:T(8,128)}, f32[1,32]{1,0:T(1,128)}) custom-call(bf16[48,9984]{1,0:T(8,128)(2,1)} %part_hbm.1, s32[1,48]{1,0:T(1,128)} %bitcast.8, f32[8,4992]{1,0:T(8,128)} %constant.2.clone.table_ref, bf16[128,9984]{1,0:T(8,128)(2,1)} %refs_hbm.1, f32[39,128]{1,0:T(8,128)} %bitcast.7, ...), custom_call_target="tpu_custom_call" | custom-call | tf_op jit(solution)/shard_map/pallas_call | solution.py:479
  53.0 3.5 %shard_map.94 = (f32[2496,128]{1,0:T(8,128)}, f32[1,48]{1,0:T(1,128)}, f32[16,48]{1,0:T(8,128)}, f32[1,32]{1,0:T(1,128)}) custom-call(f32[2560,128]{1,0:T(8,128)} %get-tuple-element.12.sums_in, f32[1,48]{1,0:T(1,128)} %get-tuple-element.13.evid_in, f32[16,48]{1,0:T(8,128)} %get-tuple-element.14.share_in, f32[1,32]{1,0:T(1,128)} %get-tuple-element.15.total_in), custom_call_target="tpu_custom_call" | custom-call | tf_op jit(solution)/shard_map/pallas_call | solution.py:535

commit v6 on v4

--- a/solution.py
+++ b/solution.py
@@ -10,7 +10,7 @@
 from jax.sharding import PartitionSpec as P
 
 CLASSES = 16
-WINDOW = 3
+WINDOW = 4
 LANES = 128
 
 
@@ -51,7 +51,7 @@
     span,
     pieces,
     window,
-    part_ref,
+    part_hbm,
     shift_ref,
     table_ref,
     refs_hbm,
@@ -62,6 +62,7 @@
     share_ref,
     total_ref,
     noise2,
+    part_ref,
     shifted,
     gath,
     refbuf,
@@ -75,6 +76,7 @@
     share_in,
     totbuf,
     own_part,
+    part_sem,
     ref_sem,
     own_sem,
     z_send,
@@ -110,6 +112,8 @@
     def chunk(z):
         return pl.ds(pl.multiple_of(first_tile(z) * LANES, LANES), span)
 
+    part_copy = pltpu.make_async_copy(part_hbm, part_ref, part_sem)
+    part_copy.start()
     barrier = pltpu.get_barrier_semaphore()
 
     def greet_ptl(step):
@@ -130,6 +134,7 @@
     step_y = (step_y - 1).astype(jnp.float32)
     cos_x = jnp.where(step_x == 0.0, 1.0, table_ref[0:1, 0:LANES])
     sin_x = step_x * table_ref[1:2, 0:LANES]
+    part_copy.wait()
     for tile in range(half // LANES):
         lo = slice(tile * LANES, (tile + 1) * LANES)
         hi = slice(half + tile * LANES, half + (tile + 1) * LANES)
@@ -230,8 +235,10 @@
     for r in range(pieces):
         spread(r)
 
-    noise2[:, 0:half] = noise_ref[...]
-    noise2[:, half:width] = noise_ref[...]
+    for tile in range(half // LANES):
+        row = noise_ref[tile : tile + 1, :]
+        noise2[:, tile * LANES : (tile + 1) * LANES] = row
+        noise2[:, half + tile * LANES : half + (tile + 1) * LANES] = row
 
     ref_copy.wait()
     offset = ptl * part_cols - first_tile(ptl) * LANES
@@ -451,6 +458,7 @@
     window = WINDOW
     n_pieces = n_ptl * pieces
     vmem = pl.BlockSpec(memory_space=pltpu.VMEM)
+    far = pl.BlockSpec(memory_space=pl.ANY)
     dma = pltpu.SemaphoreType.DMA
     sums, evidence, share, total = pl.pallas_call(
         functools.partial(kernel, n_lib, n_ptl, span, pieces, window),
@@ -460,10 +468,11 @@
             jax.ShapeDtypeStruct((CLASSES, rows), jnp.float32),
             jax.ShapeDtypeStruct((1, own_total), jnp.float32),
         ),
-        in_specs=[vmem, vmem, vmem, pl.BlockSpec(memory_space=pl.ANY), vmem, vmem],
+        in_specs=[far, vmem, vmem, far, vmem, vmem],
         out_specs=(vmem, vmem, vmem, vmem),
         scratch_shapes=[
             pltpu.VMEM((1, width), jnp.float32),
+            pltpu.VMEM((rows, width), jnp.bfloat16),
             pltpu.VMEM((rows, width), jnp.bfloat16),
             pltpu.VMEM((n_ptl, n_lib, rows, span), jnp.bfloat16),
             pltpu.VMEM((projections, span), jnp.bfloat16),
@@ -477,6 +486,7 @@
             pltpu.VMEM((n_lib - 1, CLASSES, rows), jnp.float32),
             pltpu.VMEM((8, projections), jnp.float32),
             pltpu.VMEM((projections, span), jnp.float32),
+            dma,
             dma,
             dma,
             dma((n_pieces - pieces,)),
@@ -502,10 +512,9 @@
         shifts[None, :],
         trig_table(width // 2),
         references,
-        inv_noise[None, :],
+        inv_noise.reshape(-1, LANES),
         proj_class[None, :],
     )
-    far = pl.BlockSpec(memory_space=pl.ANY)
     sums, evidence, share, total = pl.pallas_call(
         functools.partial(finish, n_ptl),
         out_shape=(

time: 58.1 us -> 56.2 us (0.967)
  local copies, waits for them, and re-layouts: 1.35 us -> 0 us
    broadcast_in_dim x1 -> x0, local copies, waits for them, and re-layouts: 1.35 us -> none  [on_device(): inv_noise[None, :]]
where the time goes in v6:
time: 56.2 us; the launch traced here: 56 us
  Pallas kernels  55.3 us (98%)
  between operations  0.64 us (1%)
    pallas_call x1, Pallas kernels, on_device(): pl.pallas_call(functools.partial(kernel, n_lib, n_ptl, span, pieces, wind...  52.4 us
    pallas_call x1, Pallas kernels, on_device(): pl.pallas_call(functools.partial(finish, n_ptl), out_shape=(jax.ShapeDtyp...  2.98 us

profile of v6, /device:TPU:0, one launch (start us, length us, event | category | flops | bytes accessed | tf_op | source)
XLA Modules:
  0.0 56.0 jit_solution(8309603786451289826)
XLA Ops:
  0.6 52.4 %shard_map.93 = (f32[2560,128]{1,0:T(8,128)}, f32[1,48]{1,0:T(1,128)}, f32[16,48]{1,0:T(8,128)}, f32[1,32]{1,0:T(1,128)}) custom-call(bf16[48,9984]{1,0:T(8,128)(2,1)} %part_hbm.1, s32[1,48]{1,0:T(1,128)} %bitcast.8, f32[8,4992]{1,0:T(8,128)} %constant.2.clone.table_ref, bf16[128,9984]{1,0:T(8,128)(2,1)} %refs_hbm.1, f32[39,128]{1,0:T(8,128)} %bitcast.7, ...), custom_call_target="tpu_custom_call" | custom-call | tf_op jit(solution)/shard_map/pallas_call | solution.py:463
  53.0 3.0 %shard_map.94 = (f32[2496,128]{1,0:T(8,128)}, f32[1,48]{1,0:T(1,128)}, f32[16,48]{1,0:T(8,128)}, f32[1,32]{1,0:T(1,128)}) custom-call(f32[2560,128]{1,0:T(8,128)} %get-tuple-element.12.sums_in, f32[1,48]{1,0:T(1,128)} %get-tuple-element.13.evid_in, f32[16,48]{1,0:T(8,128)} %get-tuple-element.14.share_in, f32[1,32]{1,0:T(1,128)} %get-tuple-element.15.total_in), custom_call_target="tpu_custom_call" | custom-call | tf_op jit(solution)/shard_map/pallas_call | solution.py:518
